TPU v7x, 256 devices: a whole 4x4x8 slice. The times are simulated.
256 devices in a mesh: dp: 8 (over z), space: 8 (over x, core), tensor: 4 (over y).
Axes of the slice: x: 4, y: 4, z: 8, core: 2. Of those that a mesh axis runs over, the one named last changes fastest.
Arguments:
- feat_policy: bfloat16 [8, 2, 320, 32, 128], P('dp', None, 'tensor', 'space'), may hold values from -6 to 6
- feat_ref: bfloat16 [8, 2, 320, 32, 128], P('dp', None, 'tensor', 'space'), may hold values from -6 to 6
- noise: float32 [8, 2, 4, 32, 128], P('dp', None, None, 'space'), may hold values from -6 to 6
- w1_policy: bfloat16 [9, 320, 320], P(None, 'tensor'), may hold values from -0.109375 to 0.109375
- w1_ref: bfloat16 [9, 320, 320], P(None, 'tensor'), may hold values from -0.109375 to 0.109375
- b1_policy: float32 [320], P('tensor'), may hold values from -3 to 3
- b1_ref: float32 [320], P('tensor'), may hold values from -3 to 3
- gn_gain_policy: float32 [320], P('tensor'), may hold values from 0.25 to 1.75
- gn_bias_policy: float32 [320], P('tensor'), may hold values from -3 to 3
- gn_gain_ref: float32 [320], P('tensor'), may hold values from 0.25 to 1.75
- gn_bias_ref: float32 [320], P('tensor'), may hold values from -3 to 3
- w2_policy: bfloat16 [9, 4, 320], P(None, None, 'tensor'), may hold values from -0.109375 to 0.109375
- w2_ref: bfloat16 [9, 4, 320], P(None, None, 'tensor'), may hold values from -0.109375 to 0.109375
- time_table: float32 [1000, 320], P(None, 'tensor'), may hold values from -3 to 3
- timestep: int32 [8], P('dp'), may hold values from 0 to 999
- winner: int32 [8], P('dp'), may hold values from 0 to 1
Outputs:
- logits: float32 [8], P('dp')
- grad_w1: float32 [9, 320, 320], P(None, 'tensor', ('dp', 'space'))
- grad_w2: float32 [9, 4, 320], P(None, None, 'tensor')
All inputs are finite; a program needn't handle non-finite values.
Results may differ from a plain program's by a relative error of at most 0.0068.
Values may be sent and summed in bfloat16 or wider, within the bound.
No kernel may reach another device: no remote copies, remote signals or barrier semaphores. Data moves between devices by JAX's collectives and lax.ppermute only.
A program may use at most 64 MiB of HBM per device.

v0:
```python
import jax
import jax.numpy as jnp
from jax import lax
from jax.sharding import PartitionSpec as P

C = 320
GROUPS = 32
dpo_beta = 500.0
norm_eps = 1e-05


def with_halo(cells, sides, width):
    for axis, dim in sides:
        count = lax.axis_size(axis)
        ends = count - 1
        head = lax.slice_in_dim(cells, 0, width, axis=dim)
        tail = lax.slice_in_dim(cells, cells.shape[dim] - width, cells.shape[dim], axis=dim)
        cells = jnp.concatenate(
            [
                lax.ppermute(tail, axis, [(i, (i + 1) % count) for i in range(ends)]),
                cells,
                lax.ppermute(head, axis, [((i + 1) % count, i) for i in range(ends)]),
            ],
            axis=dim,
        )
    return cells


def to_kernel(weights):
    return weights.reshape(3, 3, weights.shape[1], weights.shape[2]).transpose(2, 3, 0, 1)


def flip_kernel(weights):
    shaped = weights.reshape(3, 3, weights.shape[1], weights.shape[2])[::-1, ::-1]
    return shaped.transpose(3, 2, 0, 1)


def conv_rows(inputs, kernel):
    return lax.conv_general_dilated(
        inputs,
        kernel,
        (1, 1),
        ((0, 0), (1, 1)),
        dimension_numbers=("NCHW", "OIHW", "NCHW"),
        preferred_element_type=jnp.float32,
    )


def kernel_grad(inputs, deltas):
    return lax.conv_general_dilated(
        inputs,
        deltas,
        (1, 1),
        ((0, 0), (1, 1)),
        dimension_numbers=("CNHW", "IOHW", "NCHW"),
        preferred_element_type=jnp.float32,
    )


def group_total(values, group_size):
    local_groups = values.shape[-3] // group_size
    shaped = values.reshape(values.shape[:-3] + (local_groups, group_size) + values.shape[-2:])
    return jnp.sum(shaped, axis=(-3, -2, -1))


def spread_back(stat, group_size):
    return jnp.repeat(stat, group_size, axis=-1)[..., None, None]


def body(
    feat_policy,
    feat_ref,
    noise,
    w1_policy,
    w1_ref,
    b1_policy,
    b1_ref,
    gn_gain_policy,
    gn_bias_policy,
    gn_gain_ref,
    gn_bias_ref,
    w2_policy,
    w2_ref,
    time_table,
    timestep,
    winner,
):
    pair_count = feat_policy.shape[0]
    chan_local = feat_policy.shape[2]
    row_count = feat_policy.shape[3]
    col_count = feat_policy.shape[4]
    latent_chans = noise.shape[2]
    images = 2 * pair_count
    group_size = C // GROUPS
    stacked = jnp.stack(
        [
            feat_policy.reshape(images, chan_local, row_count, col_count),
            feat_ref.reshape(images, chan_local, row_count, col_count),
        ]
    )
    stacked_ext = with_halo(stacked, (("space", 3),), 1)
    onehot = (
        timestep[:, None] == jnp.arange(time_table.shape[0], dtype=jnp.int32)[None, :]
    ).astype(jnp.float32)
    shift = jnp.repeat(jnp.dot(onehot, time_table, precision=lax.Precision.HIGHEST), 2, axis=0)
    kernel_policy = to_kernel(w1_policy)
    kernel_frozen = to_kernel(w1_ref)
    zeros = jnp.zeros((images, chan_local, row_count, col_count), jnp.float32)
    block_in = lax.all_gather(stacked_ext, "tensor", axis=2, tiled=True)
    pre_policy = zeros + conv_rows(block_in[0], kernel_policy)
    pre_frozen = zeros + conv_rows(block_in[1], kernel_frozen)
    pre_policy = pre_policy + (b1_policy[None, :] + shift)[:, :, None, None]
    pre_frozen = pre_frozen + (b1_ref[None, :] + shift)[:, :, None, None]
    pre_both = jnp.stack([pre_policy, pre_frozen])
    group_count = group_size * row_count * lax.axis_size("space") * col_count
    sum_values, sum_squares = lax.psum(
        (group_total(pre_both, group_size), group_total(pre_both * pre_both, group_size)), "space"
    )
    group_mean = sum_values / group_count
    inv_std = lax.rsqrt(sum_squares / group_count - group_mean * group_mean + norm_eps)
    centered = (pre_both - spread_back(group_mean, group_size)) * spread_back(inv_std, group_size)
    gains = jnp.stack([gn_gain_policy, gn_gain_ref])[:, None, :, None, None]
    offsets = jnp.stack([gn_bias_policy, gn_bias_ref])[:, None, :, None, None]
    normed = centered * gains + offsets
    hidden = jax.nn.silu(normed).astype(jnp.bfloat16)
    hidden_ext = with_halo(hidden, (("space", 3),), 1)
    part_policy = conv_rows(hidden_ext[0], to_kernel(w2_policy))
    part_frozen = conv_rows(hidden_ext[1], to_kernel(w2_ref))
    noise_img = noise.reshape(images, latent_chans, row_count, col_count)
    cell_total = latent_chans * row_count * lax.axis_size("space") * col_count
    share_policy, share_frozen = (
        lax.psum_scatter(part_policy, "tensor", scatter_dimension=1, tiled=True),
        lax.psum_scatter(part_frozen, "tensor", scatter_dimension=1, tiled=True),
    )
    per_share = latent_chans // lax.axis_size("tensor")
    noise_own = lax.dynamic_slice_in_dim(
        noise_img, lax.axis_index("tensor") * per_share, per_share, 1
    )
    squares = jnp.stack(
        [
            jnp.sum((share_policy - noise_own) ** 2, axis=(1, 2, 3)),
            jnp.sum((share_frozen - noise_own) ** 2, axis=(1, 2, 3)),
        ]
    )
    errors = lax.psum(squares, ("space", "tensor"))
    residual = share_policy - noise_own
    errors = (errors / cell_total).reshape(2, pair_count, 2)
    pair_sign = 1.0 - 2.0 * winner.astype(jnp.float32)
    logits = (
        -0.5
        * dpo_beta
        * pair_sign
        * (errors[0, :, 0] - errors[0, :, 1] - (errors[1, :, 0] - errors[1, :, 1]))
    )
    weight = jax.nn.sigmoid(-logits)
    scaled = (
        (dpo_beta * weight * pair_sign / cell_total)[:, None]
        * jnp.array([1.0, -1.0], jnp.float32)[None, :]
    ).reshape(images)
    dpred = (scaled[:, None, None, None] * residual).astype(jnp.bfloat16)
    dpred = lax.all_gather(dpred, "tensor", axis=1, tiled=True)
    dpred_ext = with_halo(dpred, (("space", 2),), 1)
    head_local = kernel_grad(hidden_ext[0], dpred)
    head_local = head_local.transpose(2, 3, 1, 0).reshape(9, latent_chans, chan_local)
    grad_w2 = lax.psum(head_local, ("dp", "space"))
    dhidden = conv_rows(dpred_ext, flip_kernel(w2_policy))
    normed_policy = normed[0]
    centered_policy = centered[0]
    gate_value = jax.nn.sigmoid(normed_policy)
    gnorm = (
        dhidden
        * gate_value
        * (1.0 + normed_policy * (1.0 - gate_value))
        * gn_gain_policy[None, :, None, None]
    )
    first_sum, second_sum = lax.psum(
        (group_total(gnorm, group_size), group_total(gnorm * centered_policy, group_size)), "space"
    )
    first_mean = spread_back(first_sum / group_count, group_size)
    second_mean = spread_back(second_sum / group_count, group_size)
    delta = (
        spread_back(inv_std[0], group_size) * (gnorm - first_mean - centered_policy * second_mean)
    ).astype(jnp.bfloat16)
    body_local = kernel_grad(lax.all_gather(stacked_ext[0], "tensor", axis=1, tiled=True), delta)
    body_local = body_local.transpose(2, 3, 1, 0).reshape(9, chan_local, body_local.shape[0])
    grad_w1 = lax.psum_scatter(body_local, ("dp", "space"), scatter_dimension=2, tiled=True)
    return (logits, grad_w1, grad_w2)


def solution(mesh):
    in_specs = (
        P("dp", None, "tensor", "space", None),
        P("dp", None, "tensor", "space", None),
        P("dp", None, None, "space", None),
        P(None, "tensor", None),
        P(None, "tensor", None),
        P("tensor"),
        P("tensor"),
        P("tensor"),
        P("tensor"),
        P("tensor"),
        P("tensor"),
        P(None, None, "tensor"),
        P(None, None, "tensor"),
        P(None, "tensor"),
        P("dp"),
        P("dp"),
    )
    out_specs = (P("dp"), P(None, "tensor", ("dp", "space")), P(None, None, "tensor"))
    return jax.shard_map(body, mesh=mesh, in_specs=in_specs, out_specs=out_specs, check_vma=False)
```

profile of v0, /device:TPU:8, one launch (start us, length us, event | category | flops | bytes accessed | tf_op | source)
XLA Modules:
  0.0 516.6 jit_solution(16194882127117866804)
XLA Ops:
  7.3 1.2 copy_dynamic-update-slice_fusion.1
  8.5 1.1 copy_dynamic-update-slice_fusion
  9.8 1.7 collective-permute-start
  11.5 1.3 collective-permute-start.1
  12.8 3.1 collective-permute-done.1
  16.0 1.5 pad_maximum_fusion.2
  19.8 1.9 slice.99
  21.6 32.6 %all-gather.3.cloned.1.call-done = bf16[2,2,320,6,128]{4,1,3,0,2:T(2,128)(2,1)} async-done(((bf16[2,2,80,6,128]{4,1,3,0,2:T(2,128)(2,1)}), bf16[2,2,320,6,128]{4,1,3,0,2:T(2,128)(2,1)}) %all-gather.3.cloned.1.call-update) | async-done | bytes 1966096 | tf_op jit(solution)/shard_map/all_gather | solution.py:109
  54.3 3.3 slice_bitcast_fusion.1
  57.6 3.8 copy.156
  61.4 1.0 pad.clone
  62.5 1.4 fusion.2
  63.9 2.1 fusion.13
  66.3 2.0 copy.157
  68.3 1.0 pad.2.clone
  69.5 1.4 fusion.3
  70.9 2.1 fusion.19
  73.3 1.1 copy_bitcast_fusion.1
  75.2 14.6 %all-reduce.4 = (f32[2,2,8]{2,1,0:T(2,128)S(1)}, f32[2,2,8]{2,1,0:T(2,128)S(1)}) all-reduce(f32[2,2,8]{2,1,0:T(2,128)S(1)} %get-tuple-element.4, f32[2,2,8]{2,1,0:T(2,128)S(1)} %get-tuple-element.3), channel_id=1, replica_groups=mesh['dp'=8,'space'=8,'tensor'=4] {'space'}, use_global_device_ids=true, to_apply=%region_3.0 | all-reduce | flops 64 | bytes 512 | tf_op jit(solution)/shard_map/psum | solution.py:116
  90.1 2.5 fusion.25
  92.8 1.3 collective-permute-start.2
  94.1 1.3 collective-permute-start.3
  95.4 14.1 %all-gather = bf16[1,2,320,6,128]{4,1,3,0,2:T(2,128)(2,1)S(1)} all-gather(bf16[1,2,80,6,128]{4,1,3,0,2:T(2,128)(2,1)S(1)} %copy-done.2), channel_id=2, replica_groups=mesh['dp'=8,'space'=8,'tensor'=4] {'tensor'}, dimensions={2}, use_global_device_ids=true | all-gather | bytes 1228800 | tf_op jit(solution)/shard_map/all_gather | solution.py:184
  109.5 1.4 pad_maximum_fusion
  110.9 1.3 slice_bitcast_fusion.4
  112.7 4.0 convolution_select_fusion.1
  116.7 1.1 copy.139
  117.9 1.4 pad.4
  119.4 4.7 convolution_select_fusion.2
  124.1 1.1 copy.135
  125.4 15.8 %all-reduce.5 = (f32[2,4,4,128]{3,2,0,1:T(4,128)S(1)}, f32[2,4,4,128]{3,2,0,1:T(4,128)S(1)}) all-reduce(f32[2,4,4,128]{3,2,0,1:T(4,128)S(1)} %copy.136, f32[2,4,4,128]{3,2,0,1:T(4,128)S(1)} %copy.140), channel_id=3, replica_groups=mesh['dp'=8,'space'=8,'tensor'=4] {'tensor'}, use_global_device_ids=true, to_apply=%region_4.5.clone | all-reduce | flops 8192 | bytes 65536
  141.1 1.4 multiply_reduce_fusion.2
  142.6 3.2 copy.141
  145.8 64.8 %psum.44 = f32[2,2]{1,0:T(2,128)S(1)} all-reduce(f32[2,2]{1,0:T(2,128)S(1)} %pad_maximum_fusion.5), channel_id=1, replica_groups=mesh['dp'=8,'space'=8,'tensor'=4] {'space','tensor'}, use_global_device_ids=true, to_apply=%region_8.9 | all-reduce | flops 4 | bytes 32 | tf_op jit(solution)/shard_map/psum | solution.py:145
  213.9 0.7 broadcast_multiply_fusion.3
  214.5 1.4 multiply_convert_fusion.2
  215.9 10.2 %all_gather.11 = bf16[2,4,4,128]{3,2,0,1:T(4,128)(2,1)S(1)} all-gather(bf16[2,1,4,128]{3,2,0,1:T(4,128)(2,1)S(1)} %multiply_convert_fusion.2), channel_id=1, replica_groups=mesh['dp'=8,'space'=8,'tensor'=4] {'tensor'}, dimensions={1}, use_global_device_ids=true | all-gather | bytes 10240 | tf_op jit(solution)/shard_map/all_gather | solution.py:161
  226.1 1.3 collective-permute-start.4
  227.4 1.3 collective-permute-start.5
  228.9 1.6 collective-permute-done.5
  231.9 0.9 copy-done.1
  232.8 1.4 fusion.63
  234.5 12.8 %all-reduce.3 = (f32[2,8]{1,0:T(2,128)S(1)}, f32[2,8]{1,0:T(2,128)S(1)}) all-reduce(f32[2,8]{1,0:T(2,128)S(1)} %reduce_sum.77, f32[2,8]{1,0:T(2,128)S(1)} %reduce_sum.74), channel_id=1, replica_groups=mesh['dp'=8,'space'=8,'tensor'=4] {'space'}, use_global_device_ids=true, to_apply=%region_14.15 | all-reduce | flops 32 | bytes 256 | tf_op jit(solution)/shard_map/psum | solution.py:176
  247.6 7.1 %fusion.22 = f32[3,3,80,320]{2,3,1,0:T(8,128)} fusion(bf16[1,2,320,6,128]{2,1,4,3,0:T(2,128)(2,1)} %copy.141, f32[2,80,4,128]{1,0,3,2:T(2,128)S(1)} %get-tuple-element.15, f32[2,2,80,4,128]{2,1,4,3,0:T(2,128)S(1)} %get-tuple-element.18, f32[2,80]{1,0:T(2,128)S(1)} %mul.129, f32[2,80]{1,0:T(2,128)S(1)} %sub.65, f32[2,80]{1,0:T(2,128)S(1)} %mul.114), kind=kOutput, calls=%fused_computation.16 | convolution fusion | flops 469811200 | bytes 2956288 | tf_op jit(solution)/shard_map/transpose | solution.py:185
  254.8 0.7 copy-done.14
  257.0 1.6 fusion.44
  258.6 248.5 %psum.47 = f32[9,4,80]{2,1,0:T(4,128)} all-reduce(f32[9,4,80]{2,1,0:T(4,128)S(1)} %bitcast.159), channel_id=1, replica_groups=mesh['dp'=8,'space'=8,'tensor'=4] {'dp','space'}, use_global_device_ids=true, to_apply=%region_16.17 | all-reduce | flops 2880 | bytes 23040 | tf_op jit(solution)/shard_map/psum | solution.py:165
  507.1 1.5 constant_dynamic-slice_fusion
  (107 shorter events, 7.8 us)
Async XLA Ops:
  7.2 56.8 %copy-start = (bf16[9,80,320]{2,1,0:T(8,128)(2,1)S(1)}, bf16[9,80,320]{2,1,0:T(8,128)(2,1)}, u32[]{:S(2)}) copy-start(bf16[9,80,320]{2,1,0:T(8,128)(2,1)} %param.20) | copy-start | bytes 1382404
  7.2 11.7 %copy-start.15 = (u32[256]{0:T(256)S(1)}, u32[256]{0:T(256)}, u32[]{:S(2)}) copy-start(u32[256]{0:T(256)} %constant.73) | copy-start | bytes 3076
  7.2 12.3 %copy-start.4 = (f32[80]{0:T(128)S(1)}, f32[80]{0:T(128)}, u32[]{:S(2)}) copy-start(f32[80]{0:T(128)} %param.24) | copy-start | bytes 964
  7.2 12.3 %copy-start.8 = (f32[80]{0:T(128)S(1)}, f32[80]{0:T(128)}, u32[]{:S(2)}) copy-start(f32[80]{0:T(128)} %param.26) | copy-start | bytes 964
  7.2 12.3 %copy-start.10 = (f32[80]{0:T(128)S(1)}, f32[80]{0:T(128)}, u32[]{:S(2)}) copy-start(f32[80]{0:T(128)} %param.25) | copy-start | bytes 964
  7.2 12.3 %copy-start.9 = (f32[80]{0:T(128)S(1)}, f32[80]{0:T(128)}, u32[]{:S(2)}) copy-start(f32[80]{0:T(128)} %param.27) | copy-start | bytes 964
  7.2 12.3 %copy-start.6 = (f32[80]{0:T(128)S(1)}, f32[80]{0:T(128)}, u32[]{:S(2)}) copy-start(f32[80]{0:T(128)} %param.22) | copy-start | bytes 964
  7.2 12.3 %copy-start.7 = (f32[80]{0:T(128)S(1)}, f32[80]{0:T(128)}, u32[]{:S(2)}) copy-start(f32[80]{0:T(128)} %param.23) | copy-start | bytes 964
  7.3 12.3 %copy-start.3 = (f32[1000,80]{0,1:T(8,128)S(1)}, f32[1000,80]{0,1:T(8,128)}, u32[]{:S(2)}) copy-start(f32[1000,80]{0,1:T(8,128)} %param.30) | copy-start | bytes 960004
  7.3 47.0 %all-gather.3.cloned.1.call-start = ((), (), s32[]{:S(2)}) async-start(), calls=%async_computation | async-start | bytes 2457600 | tf_op jit(solution)/shard_map/all_gather | solution.py:109
  9.8 3.1 collective-permute-start
  11.5 4.4 collective-permute-start.1
  17.5 489.6 %all-reduce.8.cloned.1.call-start = ((), (), s32[]{:S(2)}) async-start(), calls=%async_computation.1 | async-start | bytes 2949120
  62.5 1.4 copy-start.16
  69.5 1.4 copy-start.11
  90.1 5.3 %copy-start.2 = (bf16[1,2,80,6,128]{4,1,3,0,2:T(2,128)(2,1)S(1)}, bf16[1,2,80,6,128]{4,1,3,0,2:T(2,128)(2,1)}, u32[]{:S(2)}) copy-start(bf16[1,2,80,6,128]{4,1,3,0,2:T(2,128)(2,1)} %slice.99) | copy-start | bytes 737284
  92.8 16.7 %collective-permute-start.2 = (bf16[2,2,80,1,128]{2,1,4,3,0:T(2,128)(2,1)S(1)}, bf16[2,2,80,1,128]{2,1,4,3,0:T(2,128)(2,1)S(1)}, u32[]{:S(2)}, u32[]{:S(2)}) collective-permute-start(bf16[2,2,80,1,128]{2,1,4,3,0:T(2,128)(2,1)S(1)} %get-tuple-element.23), channel_id=1, source_target_pairs={{0,4},{4,8},{8,12},{12,16},{16,20},{20,24},{24,28},{1,5},{5,9},{9,... | collective-permute-start | bytes 245768 | tf_op jit(solution)/shard_map/ppermute | solution.py:20
  94.1 15.4 %collective-permute-start.3 = (bf16[2,2,80,1,128]{2,1,4,3,0:T(2,128)(2,1)S(1)}, bf16[2,2,80,1,128]{2,1,4,3,0:T(2,128)(2,1)S(1)}, u32[]{:S(2)}, u32[]{:S(2)}) collective-permute-start(bf16[2,2,80,1,128]{2,1,4,3,0:T(2,128)(2,1)S(1)} %get-tuple-element.24), channel_id=1, source_target_pairs={{4,0},{8,4},{12,8},{16,12},{20,16},{24,20},{28,24},{5,1},{9,5},{13... | collective-permute-start | bytes 245768 | tf_op jit(solution)/shard_map/ppermute | solution.py:22
  110.9 1.8 copy-start.12
  142.6 88.6 %copy-start.13 = (bf16[9,4,80]{2,1,0:T(4,128)(2,1)S(1)}, bf16[9,4,80]{2,1,0:T(4,128)(2,1)}, u32[]{:S(2)}) copy-start(bf16[9,4,80]{2,1,0:T(4,128)(2,1)} %param.28) | copy-start | bytes 17284
  142.6 88.6 %copy-start.17 = (pred[16,17]{0,1:T(8,128)(4,1)S(1)}, pred[16,17]{0,1:T(8,128)(4,1)}, u32[]{:S(2)}) copy-start(pred[16,17]{0,1:T(8,128)(4,1)} %constant.66) | copy-start | bytes 820
  226.1 2.8 collective-permute-start.4
  227.4 3.1 collective-permute-start.5
  231.6 1.2 copy-start.1
  231.6 1.2 copy-start.5
  254.7 0.7 copy-start.14
Sparse Core Ops, SparseCore 0:
  17.6 36.5 all-gather.2
  254.9 188.4 all-reduce.7
where the time goes:
time: 518 us; the launch traced here: 517 us
  blocking collectives  381 us (74%)
  waiting for transfers between devices  37.4 us (7%)
  local copies, waits for them, and re-layouts  33.8 us (7%)
  matrix products  22.3 us (4%)
  between operations  20.4 us (4%)
  other arithmetic  13.8 us (3%)
  starting transfers between devices  8.29 us (2%)
    psum x1, blocking collectives, body(): grad_w2 = lax.psum(head_local, ('dp', 'space'))  249 us
    psum x1, blocking collectives, body(): errors = lax.psum(squares, ('space', 'tensor'))  64.8 us
    all_gather x1, waiting for transfers between devices, body(): block_in = lax.all_gather(stacked_ext, 'tensor', axis=2, tiled=True)  32.6 us
    unnamed x1, blocking collectives  15.8 us
    psum x1, blocking collectives, body(): lax.psum((group_total(pre_both, group_size), group_total(pre_both * pre_b...  14.6 us
    all_gather x1, blocking collectives, body(): lax.all_gather(stacked_ext[0], 'tensor', axis=1, tiled=True)  14.1 us
    conv_general_dilated x5, matrix products, conv_rows(): lax.conv_general_dilated(inputs, kernel, (1, 1), ((0, 0), (1, 1)), dimens...  13.3 us
    psum x1, blocking collectives, body(): lax.psum((group_total(gnorm, group_size), group_total(gnorm * centered_po...  12.8 us
  transfers between devices with their start and end apart: 8, of which 3 were waited for; matrix products, arithmetic and copies ran while one was open for 1% of the time, Pallas kernels for 0%

commit v1 on v0

--- a/solution.py
+++ b/solution.py
@@ -162,7 +162,7 @@
     dpred_ext = with_halo(dpred, (("space", 2),), 1)
     head_local = kernel_grad(hidden_ext[0], dpred)
     head_local = head_local.transpose(2, 3, 1, 0).reshape(9, latent_chans, chan_local)
-    grad_w2 = lax.psum(head_local, ("dp", "space"))
+    grad_w2 = jnp.sum(lax.all_gather(head_local, ("dp", "space")), axis=0)
     dhidden = conv_rows(dpred_ext, flip_kernel(w2_policy))
     normed_policy = normed[0]
     centered_policy = centered[0]

time: 518 us -> 454 us (0.88)
  blocking collectives: 381 us -> 183 us
  waiting for transfers between devices: 37.4 us -> 171 us
    psum x1 -> x0, blocking collectives: 249 us -> none  [body(): grad_w2 = lax.psum(head_local, ('dp', 'space'))]
    unnamed x3, waiting for transfers between devices: 0.03 us -> 135 us
    all_gather x0 -> x1, blocking collectives: none -> 50.7 us  [body(): grad_w2 = jnp.sum(lax.all_gather(head_local, ('dp', 'space')), axis=0)]
  transfers between devices with their start and end apart: 8 -> 8, of which waited for: 3 -> 4; matrix products, arithmetic and copies ran while one was open for 1% -> 1% of each run, Pallas kernels for 0% -> 0%
where the time goes in v1:
time: 454 us
  blocking collectives  183 us (40%)
  waiting for transfers between devices  171 us (38%)
  local copies, waits for them, and re-layouts  33.2 us (7%)
  matrix products  22.4 us (5%)
  between operations  20.5 us (5%)
  other arithmetic  15.4 us (3%)
  starting transfers between devices  8.29 us (2%)
    unnamed x3, waiting for transfers between devices  135 us
    psum x1, blocking collectives, body(): errors = lax.psum(squares, ('space', 'tensor'))  64.8 us
    all_gather x1, blocking collectives, body(): grad_w2 = jnp.sum(lax.all_gather(head_local, ('dp', 'space')), axis=0)  50.7 us
    all_gather x1, waiting for transfers between devices, body(): block_in = lax.all_gather(stacked_ext, 'tensor', axis=2, tiled=True)  31.3 us
    unnamed x1, blocking collectives  15.8 us
    psum x1, blocking collectives, body(): lax.psum((group_total(pre_both, group_size), group_total(pre_both * pre_b...  14.6 us
    all_gather x1, blocking collectives, body(): lax.all_gather(stacked_ext[0], 'tensor', axis=1, tiled=True)  14.1 us
    conv_general_dilated x5, matrix products, conv_rows(): lax.conv_general_dilated(inputs, kernel, (1, 1), ((0, 0), (1, 1)), dimens...  13.3 us
  transfers between devices with their start and end apart: 8, of which 4 were waited for; matrix products, arithmetic and copies ran while one was open for 1% of the time, Pallas kernels for 0%

profile of v1, /device:TPU:8, one launch (start us, length us, event | category | flops | bytes accessed | tf_op | source)
XLA Modules:
  0.0 453.6 jit_solution(16331643061071486178)
XLA Ops:
  7.3 1.2 copy_dynamic-update-slice_fusion.1
  8.5 1.1 copy_dynamic-update-slice_fusion
  9.8 1.7 collective-permute-start
  11.5 1.3 collective-permute-start.1
  12.8 3.1 collective-permute-done.1
  16.0 1.5 pad_maximum_fusion.2
  21.1 1.9 slice.99
  22.9 31.3 %all-gather.3.cloned.1.call-done = bf16[2,2,320,6,128]{4,1,3,0,2:T(2,128)(2,1)} async-done(((bf16[2,2,80,6,128]{4,1,3,0,2:T(2,128)(2,1)}), bf16[2,2,320,6,128]{4,1,3,0,2:T(2,128)(2,1)}) %all-gather.3.cloned.1.call-update) | async-done | bytes 1966096 | tf_op jit(solution)/shard_map/all_gather | solution.py:109
  54.3 3.3 slice_bitcast_fusion.1
  57.6 3.8 copy.156
  61.4 1.0 pad.clone
  62.6 1.4 fusion.2
  64.0 2.1 fusion.13
  66.3 2.0 copy.157
  68.3 1.0 pad.2.clone
  69.5 1.4 fusion.3
  70.9 2.1 fusion.19
  73.3 1.1 copy_bitcast_fusion.1
  75.2 14.6 %all-reduce.4 = (f32[2,2,8]{2,1,0:T(2,128)S(1)}, f32[2,2,8]{2,1,0:T(2,128)S(1)}) all-reduce(f32[2,2,8]{2,1,0:T(2,128)S(1)} %get-tuple-element.4, f32[2,2,8]{2,1,0:T(2,128)S(1)} %get-tuple-element.3), channel_id=1, replica_groups=mesh['dp'=8,'space'=8,'tensor'=4] {'space'}, use_global_device_ids=true, to_apply=%region_3.0 | all-reduce | flops 64 | bytes 512 | tf_op jit(solution)/shard_map/psum | solution.py:116
  90.1 2.5 fusion.25
  92.8 1.3 collective-permute-start.2
  94.1 1.3 collective-permute-start.3
  95.4 14.1 %all-gather = bf16[1,2,320,6,128]{4,1,3,0,2:T(2,128)(2,1)S(1)} all-gather(bf16[1,2,80,6,128]{4,1,3,0,2:T(2,128)(2,1)S(1)} %copy-done.2), channel_id=2, replica_groups=mesh['dp'=8,'space'=8,'tensor'=4] {'tensor'}, dimensions={2}, use_global_device_ids=true | all-gather | bytes 1228800 | tf_op jit(solution)/shard_map/all_gather | solution.py:184
  109.5 1.4 pad_maximum_fusion
  110.9 1.3 slice_bitcast_fusion.4
  112.7 4.0 convolution_select_fusion.1
  116.7 1.1 copy.139
  117.9 1.4 pad.4
  119.5 4.7 %convolution_select_fusion.2 = f32[4,16,17,4]{1,3,2,0:T(4,128)} fusion(bf16[3,3,4,80]{3,2,1,0:T(4,128)(2,1)} %bitcast.168, bf16[80,6,2,7,2]{0,3,2,4,1:T(8,128)(2,1)S(1)} %slice.94, bf16[80,6,2,8,17]{0,3,2,4,1:T(8,128)(2,1)S(1)} %copy.134, pred[16,17]{0,1:T(8,128)(4,1)} %constant.66), kind=kOutput, calls=%fused_computation.19 | convolution fusion | flops 7146752 | bytes 311440 | tf_op jit(solution)/shard_map/conv_general_dilated | solution.py:39
  124.2 1.1 copy.135
  125.4 15.8 %all-reduce.5 = (f32[2,4,4,128]{3,2,0,1:T(4,128)S(1)}, f32[2,4,4,128]{3,2,0,1:T(4,128)S(1)}) all-reduce(f32[2,4,4,128]{3,2,0,1:T(4,128)S(1)} %copy.136, f32[2,4,4,128]{3,2,0,1:T(4,128)S(1)} %copy.140), channel_id=3, replica_groups=mesh['dp'=8,'space'=8,'tensor'=4] {'tensor'}, use_global_device_ids=true, to_apply=%region_4.5.clone | all-reduce | flops 8192 | bytes 65536
  141.1 1.4 multiply_reduce_fusion.2
  142.6 3.2 copy.141
  145.8 64.8 %psum.37 = f32[2,2]{1,0:T(2,128)S(1)} all-reduce(f32[2,2]{1,0:T(2,128)S(1)} %pad_maximum_fusion.5), channel_id=1, replica_groups=mesh['dp'=8,'space'=8,'tensor'=4] {'space','tensor'}, use_global_device_ids=true, to_apply=%region_8.9 | all-reduce | flops 4 | bytes 32 | tf_op jit(solution)/shard_map/psum | solution.py:145
  214.6 1.4 multiply_convert_fusion.2
  216.0 10.2 %all_gather.14 = bf16[2,4,4,128]{3,2,0,1:T(4,128)(2,1)S(1)} all-gather(bf16[2,1,4,128]{3,2,0,1:T(4,128)(2,1)S(1)} %multiply_convert_fusion.2), channel_id=1, replica_groups=mesh['dp'=8,'space'=8,'tensor'=4] {'tensor'}, dimensions={1}, use_global_device_ids=true | all-gather | bytes 10240 | tf_op jit(solution)/shard_map/all_gather | solution.py:161
  226.2 1.3 collective-permute-start.4
  227.5 1.3 collective-permute-start.5
  229.3 1.2 collective-permute-done.5
  231.9 0.9 copy-done.1
  232.8 2.1 fusion.63
  235.3 12.8 %all-reduce.3 = (f32[2,8]{1,0:T(2,128)S(1)}, f32[2,8]{1,0:T(2,128)S(1)}) all-reduce(f32[2,8]{1,0:T(2,128)S(1)} %reduce_sum.86, f32[2,8]{1,0:T(2,128)S(1)} %reduce_sum.83), channel_id=1, replica_groups=mesh['dp'=8,'space'=8,'tensor'=4] {'space'}, use_global_device_ids=true, to_apply=%region_14.15 | all-reduce | flops 32 | bytes 256 | tf_op jit(solution)/shard_map/psum | solution.py:176
  248.4 7.2 %fusion.22 = f32[3,3,80,320]{2,3,1,0:T(8,128)} fusion(bf16[1,2,320,6,128]{2,1,4,3,0:T(2,128)(2,1)} %copy.141, f32[2,80,4,128]{1,0,3,2:T(2,128)} %get-tuple-element.15, f32[2,2,80,4,128]{2,1,4,3,0:T(2,128)S(1)} %get-tuple-element.18, f32[2,80]{1,0:T(2,128)S(1)} %mul.129, f32[2,80]{1,0:T(2,128)S(1)} %sub.65, f32[2,80]{1,0:T(2,128)S(1)} %mul.114), kind=kOutput, calls=%fused_computation.16 | convolution fusion | flops 469811200 | bytes 2759680 | tf_op jit(solution)/shard_map/transpose | solution.py:185
  255.6 1.6 fusion.44
  257.2 50.7 %all_gather.15 = f32[64,9,4,80]{3,2,1,0:T(4,128)S(1)} all-gather(f32[1,9,4,80]{3,2,1,0:T(4,128)S(1)} %bitcast.159), channel_id=1, replica_groups=mesh['dp'=8,'space'=8,'tensor'=4] {'dp','space'}, dimensions={0}, use_global_device_ids=true | all-gather | bytes 748800 | tf_op jit(solution)/shard_map/all_gather | solution.py:165
  307.9 0.9 reduce_sum.87
  308.8 135.3 %all-reduce.8.cloned.1.call-done = f32[9,80,320]{1,2,0:T(8,128)} async-done(((f32[9,80,320]{1,2,0:T(8,128)}), f32[9,80,320]{1,2,0:T(8,128)}) %all-reduce.8.cloned.1.call-update) | async-done | bytes 921616
  444.1 1.5 constant_dynamic-slice_fusion
  (108 shorter events, 8.4 us)
Async XLA Ops:
  7.2 56.8 %copy-start = (bf16[9,80,320]{2,1,0:T(8,128)(2,1)S(1)}, bf16[9,80,320]{2,1,0:T(8,128)(2,1)}, u32[]{:S(2)}) copy-start(bf16[9,80,320]{2,1,0:T(8,128)(2,1)} %param.20) | copy-start | bytes 1382404
  7.2 11.7 %copy-start.15 = (u32[256]{0:T(256)S(1)}, u32[256]{0:T(256)}, u32[]{:S(2)}) copy-start(u32[256]{0:T(256)} %constant.73) | copy-start | bytes 3076
  7.2 12.3 %copy-start.14 = (u32[256]{0:T(256)S(1)}, u32[256]{0:T(256)}, u32[]{:S(2)}) copy-start(u32[256]{0:T(256)} %constant.81) | copy-start | bytes 3076
  7.2 13.5 %copy-start.4 = (f32[80]{0:T(128)S(1)}, f32[80]{0:T(128)}, u32[]{:S(2)}) copy-start(f32[80]{0:T(128)} %param.24) | copy-start | bytes 964
  7.2 13.5 %copy-start.8 = (f32[80]{0:T(128)S(1)}, f32[80]{0:T(128)}, u32[]{:S(2)}) copy-start(f32[80]{0:T(128)} %param.26) | copy-start | bytes 964
  7.2 13.5 %copy-start.10 = (f32[80]{0:T(128)S(1)}, f32[80]{0:T(128)}, u32[]{:S(2)}) copy-start(f32[80]{0:T(128)} %param.25) | copy-start | bytes 964
  7.2 13.5 %copy-start.9 = (f32[80]{0:T(128)S(1)}, f32[80]{0:T(128)}, u32[]{:S(2)}) copy-start(f32[80]{0:T(128)} %param.27) | copy-start | bytes 964
  7.2 13.6 %copy-start.6 = (f32[80]{0:T(128)S(1)}, f32[80]{0:T(128)}, u32[]{:S(2)}) copy-start(f32[80]{0:T(128)} %param.22) | copy-start | bytes 964
  7.3 13.6 %copy-start.7 = (f32[80]{0:T(128)S(1)}, f32[80]{0:T(128)}, u32[]{:S(2)}) copy-start(f32[80]{0:T(128)} %param.23) | copy-start | bytes 964
  7.3 13.6 %copy-start.3 = (f32[1000,80]{0,1:T(8,128)S(1)}, f32[1000,80]{0,1:T(8,128)}, u32[]{:S(2)}) copy-start(f32[1000,80]{0,1:T(8,128)} %param.30) | copy-start | bytes 960004
  7.3 47.0 %all-gather.3.cloned.1.call-start = ((), (), s32[]{:S(2)}) async-start(), calls=%async_computation | async-start | bytes 2457600 | tf_op jit(solution)/shard_map/all_gather | solution.py:109
  9.8 3.1 collective-permute-start
  11.5 4.4 collective-permute-start.1
  17.5 426.6 %all-reduce.8.cloned.1.call-start = ((), (), s32[]{:S(2)}) async-start(), calls=%async_computation.1 | async-start | bytes 2949120
  62.5 1.4 copy-start.16
  69.5 1.4 copy-start.11
  90.1 5.3 %copy-start.2 = (bf16[1,2,80,6,128]{4,1,3,0,2:T(2,128)(2,1)S(1)}, bf16[1,2,80,6,128]{4,1,3,0,2:T(2,128)(2,1)}, u32[]{:S(2)}) copy-start(bf16[1,2,80,6,128]{4,1,3,0,2:T(2,128)(2,1)} %slice.99) | copy-start | bytes 737284
  92.8 16.7 %collective-permute-start.2 = (bf16[2,2,80,1,128]{2,1,4,3,0:T(2,128)(2,1)S(1)}, bf16[2,2,80,1,128]{2,1,4,3,0:T(2,128)(2,1)S(1)}, u32[]{:S(2)}, u32[]{:S(2)}) collective-permute-start(bf16[2,2,80,1,128]{2,1,4,3,0:T(2,128)(2,1)S(1)} %get-tuple-element.23), channel_id=1, source_target_pairs={{0,4},{4,8},{8,12},{12,16},{16,20},{20,24},{24,28},{1,5},{5,9},{9,... | collective-permute-start | bytes 245768 | tf_op jit(solution)/shard_map/ppermute | solution.py:20
  94.1 15.4 %collective-permute-start.3 = (bf16[2,2,80,1,128]{2,1,4,3,0:T(2,128)(2,1)S(1)}, bf16[2,2,80,1,128]{2,1,4,3,0:T(2,128)(2,1)S(1)}, u32[]{:S(2)}, u32[]{:S(2)}) collective-permute-start(bf16[2,2,80,1,128]{2,1,4,3,0:T(2,128)(2,1)S(1)} %get-tuple-element.24), channel_id=1, source_target_pairs={{4,0},{8,4},{12,8},{16,12},{20,16},{24,20},{28,24},{5,1},{9,5},{13... | collective-permute-start | bytes 245768 | tf_op jit(solution)/shard_map/ppermute | solution.py:22
  110.9 1.8 copy-start.12
  142.6 88.6 %copy-start.13 = (bf16[9,4,80]{2,1,0:T(4,128)(2,1)S(1)}, bf16[9,4,80]{2,1,0:T(4,128)(2,1)}, u32[]{:S(2)}) copy-start(bf16[9,4,80]{2,1,0:T(4,128)(2,1)} %param.28) | copy-start | bytes 17284
  142.6 88.6 %copy-start.17 = (pred[16,17]{0,1:T(8,128)(4,1)S(1)}, pred[16,17]{0,1:T(8,128)(4,1)}, u32[]{:S(2)}) copy-start(pred[16,17]{0,1:T(8,128)(4,1)} %constant.66) | copy-start | bytes 820
  226.2 3.1 collective-permute-start.4
  227.5 3.1 collective-permute-start.5
  231.6 1.2 copy-start.1
  231.6 1.2 copy-start.5
Sparse Core Ops, SparseCore 0:
  17.6 36.5 all-gather.2
  255.8 188.2 all-reduce.7
